TPU v7x, 32 devices: a whole 2x2x4 slice. The times are simulated.
32 devices in a mesh: dp: 16 (over z, x, core), vol: 2 (over y).
Axes of the slice: x: 2, y: 2, z: 4, core: 2. Of those that a mesh axis runs over, the one named last changes fastest.
Arguments:
- images: float32 [32, 128, 128], P(('dp', 'vol')), may hold values from -6 to 6
- contrast: bfloat16 [32, 128, 128], P(('dp', 'vol')), may hold values from -1 to 1
- volume: bfloat16 [256, 256, 256], P('vol'), may hold values from -6 to 6
- line_index: int32 [32, 4, 128], P('dp'), may hold values from 0 to 65278, as said below
- patch_weight: bfloat16 [64, 1024], replicated, may hold values from -0.75 to 0.75
- position: bfloat16 [256, 1024], replicated, may hold values from -3 to 3
- norm_gain: float32 [1024], replicated, may hold values from 0.1 to 1.9
- project_in: bfloat16 [1024, 1536], P('dp'), may hold values from -0.1875 to 0.1875
- project_out: bfloat16 [1024, 512], P('dp'), may hold values from -0.25 to 0.25
- head_weight: float32 [1024, 4], replicated, may hold values from -1.8 to 1.8
Outputs:
- errors: float32 [32, 4], P(('dp', 'vol'))
- in_gradient: float32 [1024, 1536], P('dp')
- out_gradient: float32 [1024, 512], P('dp')
- head_gradient: float32 [1024, 4], replicated
Inputs may be any that keep to these rules, and one draw needn't show every extreme that they name: line_index[i, k, r] = z * 256 + y names the plane z and row y of the volume that row r of hypothesis k of image i samples; z and y lie within 0 and 254.
All inputs are finite; a program needn't handle non-finite values.
Results may differ from a plain program's by a relative error of at most 0.038.
Values may be sent and summed in bfloat16 or wider, within the bound.
A program may use at most 64 MiB of HBM per device.

v0:
```python
import math
import jax
import jax.numpy as jnp
from jax import lax
from jax.sharding import PartitionSpec as P

HEADS = 8
HEAD_DIM = 64
PIX = 128
PATCH = 8
PATCHES = 256
K = 4
EPSILON = 1e-05


def embed_images(images, patch_weight, position):
    count = images.shape[0]
    grid = PIX // PATCH
    pieces = images.reshape(count, grid, PATCH, grid, PATCH).transpose(0, 1, 3, 2, 4)
    pieces = pieces.reshape(count * grid * grid, PATCH * PATCH).astype(jnp.bfloat16)
    mixed = jnp.dot(pieces, patch_weight, preferred_element_type=jnp.float32)
    mixed = mixed.reshape(count, grid * grid, -1) + position.astype(jnp.float32)[None]
    return mixed.reshape(count * grid * grid, -1).astype(jnp.bfloat16)


def normalize(embedded, norm_gain):
    values = embedded.astype(jnp.float32)
    center = values - jnp.mean(values, axis=1, keepdims=True)
    scale = lax.rsqrt(jnp.mean(center * center, axis=1, keepdims=True) + EPSILON)
    return (center * scale * norm_gain[None, :]).astype(jnp.bfloat16)


def attend(triple):
    count = triple.shape[0] // PATCHES
    parts = triple.reshape(count, PATCHES, 3, HEADS, HEAD_DIM).astype(jnp.float32)
    query = parts[:, :, 0]
    keys = parts[:, :, 1]
    values = parts[:, :, 2]
    scores = jnp.einsum("bqhd,bkhd->bhqk", query, keys) * HEAD_DIM ** (-0.5)
    raised = jnp.exp(scores)
    weights = (raised / jnp.sum(raised, axis=-1, keepdims=True)).astype(jnp.bfloat16)
    mixed = jnp.einsum("bhqk,bkhd->bqhd", weights.astype(jnp.float32), values)
    return mixed.reshape(count * PATCHES, HEADS * HEAD_DIM).astype(jnp.bfloat16)


def hartley(images):
    side = images.shape[1]
    freq = jnp.arange(side, dtype=jnp.int32) - side // 2
    place = jnp.arange(side, dtype=jnp.int32)
    phase = (freq[:, None] * place[None, :] % side).astype(jnp.float32) * (2.0 * math.pi / side)
    cosine = jnp.cos(phase)
    sine = jnp.sin(phase)
    highest = lax.Precision.HIGHEST
    first_cos = jnp.einsum("rn,bnm->brm", cosine, images, precision=highest)
    first_sin = jnp.einsum("rn,bnm->brm", sine, images, precision=highest)
    result = jnp.einsum("brm,cm->brc", first_cos, cosine + sine, precision=highest)
    result = result + jnp.einsum("brm,cm->brc", first_sin, cosine - sine, precision=highest)
    return result / side


def render(volume, line_index, slab_index):
    slab, side, _ = volume.shape
    table = volume.reshape(slab * side, side)
    plane = line_index // side - slab_index * slab
    inside = (plane >= 0) & (plane < slab)
    rows = jnp.clip(plane, 0, slab - 1) * side + line_index % side
    picked = jnp.take(table, rows.reshape(-1), axis=0)[:, ::2]
    picked = jnp.where(inside.reshape(-1, 1), picked.astype(jnp.float32), 0.0)
    return (picked.reshape(line_index.shape[0], -1), inside)


def local(
    images,
    contrast,
    volume,
    line_index,
    patch_weight,
    position,
    norm_gain,
    project_in,
    project_out,
    head_weight,
):
    count = images.shape[0]
    width = norm_gain.shape[0]
    highest = lax.Precision.HIGHEST
    rendered, inside = render(volume, line_index, lax.axis_index("vol"))
    spectrum = hartley(images)
    slices = lax.psum_scatter(
        rendered.astype(jnp.bfloat16), "vol", scatter_dimension=0, tiled=True
    ).astype(jnp.float32)
    slices = slices.reshape(count, K, PIX, PIX)
    misfit = contrast.astype(jnp.float32)[:, None] * slices - spectrum[:, None]
    errors = jnp.mean(misfit * misfit, axis=(2, 3))
    embedded = embed_images(images, patch_weight, position)
    normed = normalize(embedded, norm_gain)
    triple = jnp.dot(
        normed,
        lax.all_gather(project_in, "dp", axis=0, tiled=True),
        preferred_element_type=jnp.float32,
    ).astype(jnp.bfloat16)
    attended = attend(triple)
    contract_last = (((1,), (1,)), ((), ()))
    out_whole = lax.all_gather(project_out, "dp", axis=0, tiled=True)
    branch = lax.dot_general(attended, out_whole, contract_last, preferred_element_type=jnp.float32)
    layer_out = embedded.astype(jnp.float32) + branch
    pooled = jnp.mean(layer_out.reshape(count, PATCHES, width), axis=1)
    logits = jnp.dot(pooled, head_weight, precision=highest)
    raised = jnp.exp(logits)
    chances = raised / jnp.sum(raised, axis=1, keepdims=True)
    expected = jnp.sum(chances * errors, axis=1, keepdims=True)
    logit_slope = chances * (errors - expected)
    head_gradient = lax.psum(jnp.dot(pooled.T, logit_slope, precision=highest), ("dp", "vol"))
    pooled_slope = jnp.dot(logit_slope, head_weight.T, precision=highest) / PATCHES
    layer_slope = jnp.broadcast_to(pooled_slope[:, None, :], (count, PATCHES, width))
    layer_slope = layer_slope.reshape(count * PATCHES, width).astype(jnp.bfloat16)
    attended_slope = jnp.dot(layer_slope, out_whole, preferred_element_type=jnp.float32).astype(
        jnp.bfloat16
    )
    triple_slope = jax.vjp(attend, triple)[1](attended_slope)[0]
    contract_first = (((0,), (0,)), ((), ()))
    first = lax.dot_general(
        normed, triple_slope, contract_first, preferred_element_type=jnp.float32
    )
    second = lax.dot_general(
        layer_slope, attended, contract_first, preferred_element_type=jnp.float32
    )
    shard = lax.psum_scatter(
        jnp.concatenate([first, second], axis=1).astype(jnp.bfloat16),
        "dp",
        scatter_dimension=0,
        tiled=True,
    ).astype(jnp.float32)
    shard = lax.psum(shard.astype(jnp.bfloat16), "vol").astype(jnp.float32)
    split = project_in.shape[1]
    return (errors, shard[:, :split], shard[:, split:], head_gradient)


def solution(mesh):
    placed = (
        P(("dp", "vol"), None, None),
        P(("dp", "vol"), None, None),
        P("vol", None, None),
        P("dp", None, None),
        P(),
        P(),
        P(),
        P("dp", None),
        P("dp", None),
        P(),
    )
    return jax.shard_map(
        local,
        mesh=mesh,
        in_specs=placed,
        out_specs=(P(("dp", "vol"), None), P("dp", None), P("dp", None), P()),
        check_vma=False,
    )
```

profile of v0, /device:TPU:0, one launch (start us, length us, event | category | flops | bytes accessed | tf_op | source)
XLA Modules:
  0.0 261.4 jit_solution(18446166115794627641)
XLA Ops:
  8.1 0.7 fusion.38
  8.8 0.7 compare_and_fusion.1
  9.5 11.4 %gather_fusion = bf16[1024,256]{1,0:T(8,128)(2,1)S(1)} fusion(bf16[32768,256]{1,0:T(8,128)(2,1)} %bitcast.106, s32[1024]{0:T(1024)S(1)} %broadcast_clamp_fusion), kind=kCustom, calls=%fused_computation | custom fusion | bytes 1052672 | tf_op jit(solution)/shard_map/jit(_take)/gather | solution.py:67
  21.2 10.3 %slice.21 = bf16[1024,128]{1,0:T(8,128)(2,1)S(1)} slice(bf16[1024,256]{1,0:T(8,128)(2,1)S(1)} %broadcast_select_fusion), slice={[0:1024:1], [0:256:2]} | slice | bytes 524288 | tf_op jit(solution)/shard_map/slice | solution.py:67
  31.7 0.8 convert_element_type.102
  35.0 0.6 fusion.24
  35.6 0.6 convert_element_type.105
  37.5 0.6 dynamic-slice
  38.1 0.6 fusion.9
  38.7 19.9 %all-reduce.9.cloned.1.call-done = bf16[2,65536]{1,0:T(2,128)(2,1)} async-done(((bf16[2,65536]{1,0:T(2,128)(2,1)}), bf16[2,65536]{1,0:T(2,128)(2,1)}) %all-reduce.9.cloned.1.call-update) | async-done | bytes 262160
  58.6 1.8 dynamic-slice_convert_fusion
  60.4 0.6 multiply_reduce_fusion
  61.0 22.6 %all-gather.3.cloned.1.call-done = bf16[1024,1536]{1,0:T(8,128)(2,1)} async-done(((bf16[64,1536]{1,0:T(8,128)(2,1)}), bf16[1024,1536]{1,0:T(8,128)(2,1)}) %all-gather.3.cloned.1.call-update) | async-done | bytes 3145744 | tf_op jit(solution)/shard_map/all_gather | solution.py:99
  83.7 3.0 %convolution_convert_fusion.1 = bf16[256,1536]{1,0:T(8,128)(2,1)S(1)} fusion(bf16[1024,1536]{1,0:T(8,128)(2,1)} %all-gather.3.cloned.1.call-done, bf16[256,1024]{1,0:T(8,128)(2,1)S(1)} %get-tuple-element.9, f32[1024]{0:T(1024)S(1)} %copy-done.17, f32[256]{0:T(256)S(1)} %add_rsqrt_fusion, f32[256]{0:T(256)S(1)} %broadcast_multiply_fusion.2), kind=kOutput, calls=%fused_computation.5 | convolution fusion | flops 807010304 | bytes 4462592 | tf_op jit(solution)/shard_map/dot_general | solution.py:97
  88.0 1.2 convolution_convert_fusion.5
  89.3 32.9 %all-gather.5.cloned.1.call-done = bf16[1024,512]{1,0:T(8,128)(2,1)} async-done(((bf16[64,512]{1,0:T(8,128)(2,1)}), bf16[1024,512]{1,0:T(8,128)(2,1)}) %all-gather.5.cloned.1.call-update) | async-done | bytes 1048592 | tf_op jit(solution)/shard_map/all_gather | solution.py:104
  122.2 1.9 fusion.8
  124.2 0.8 fusion.64
  125.0 1.3 multiply_reduce_fusion.1
  126.3 1.2 subtract_multiply_fusion
  128.1 1.5 convolution_convert_fusion.3
  129.6 1.1 convolution_convert_fusion.4
  130.7 1.1 copy.34
  131.8 1.5 fusion.4
  133.4 0.6 convolution_bitcast_fusion
  134.0 0.6 convolution_bitcast_fusion.1
  135.6 1.2 convolution_convert_fusion
  136.8 2.6 pad_maximum_fusion
  139.5 71.4 %reduce-scatter.2.cloned.1.call-done = bf16[64,2048]{1,0:T(8,128)(2,1)} async-done(((bf16[1024,2048]{1,0:T(8,128)(2,1)}), bf16[64,2048]{1,0:T(8,128)(2,1)}) %reduce-scatter.2.cloned.1.call-update) | async-done | bytes 262160 | tf_op jit(solution)/shard_map/reduce_scatter | solution.py:128
  211.0 39.6 %psum.15 = f32[1024,4]{0,1:T(4,128)} all-reduce(f32[1024,4]{0,1:T(4,128)S(1)} %broadcast_multiply_fusion), channel_id=1, replica_groups=mesh['dp'=16,'vol'=2] {'dp','vol'}, use_global_device_ids=true, to_apply=%region_11.12 | all-reduce | flops 4096 | bytes 32768 | tf_op jit(solution)/shard_map/psum | solution.py:113
  250.6 1.7 slice.32
  252.3 1.5 slice.33
  (84 shorter events, 7.3 us)
Async XLA Ops:
  8.0 28.7 %copy-start = (bf16[64,1024]{1,0:T(8,128)(2,1)S(1)}, bf16[64,1024]{1,0:T(8,128)(2,1)}, u32[]{:S(2)}) copy-start(bf16[64,1024]{1,0:T(8,128)(2,1)} %param.14) | copy-start | bytes 393220
  8.0 50.5 %all-reduce.9.cloned.1.call-start = ((), (), s32[]{:S(2)}) async-start(), calls=%async_computation.5 | async-start | bytes 524288
  20.9 13.0 %copy-start.7 = (f32[1,128,128]{2,1,0:T(8,128)S(1)}, f32[1,128,128]{2,1,0:T(8,128)}, u32[]{:S(2)}) copy-start(f32[1,128,128]{2,1,0:T(8,128)} %param.10) | copy-start | bytes 196612
  21.0 14.6 %copy-start.8 = (bf16[1,128,128]{2,1,0:T(8,128)(2,1)S(1)}, bf16[1,128,128]{2,1,0:T(8,128)(2,1)}, u32[]{:S(2)}) copy-start(bf16[1,128,128]{2,1,0:T(8,128)(2,1)} %param.11) | copy-start | bytes 98308
  31.5 5.3 %copy-start.6 = (bf16[256,1024]{1,0:T(8,128)(2,1)S(1)}, bf16[256,1024]{1,0:T(8,128)(2,1)}, u32[]{:S(2)}) copy-start(bf16[256,1024]{1,0:T(8,128)(2,1)} %param.15) | copy-start | bytes 1572868
  32.5 51.2 %all-gather.3.cloned.1.call-start = ((), (), s32[]{:S(2)}) async-start(), calls=%async_computation.1 | async-start | bytes 3342336 | tf_op jit(solution)/shard_map/all_gather | solution.py:99
  33.1 89.2 %all-gather.5.cloned.1.call-start = ((), (), s32[]{:S(2)}) async-start(), calls=%async_computation.2 | async-start | bytes 1114112 | tf_op jit(solution)/shard_map/all_gather | solution.py:104
  33.6 177.2 %reduce-scatter.2.cloned.1.call-start = ((), (), s32[]{:S(2)}) async-start(), calls=%async_computation.3 | async-start | bytes 4456448 | tf_op jit(solution)/shard_map/reduce_scatter | solution.py:128
  34.4 3.1 %copy-start.22 = (u32[32]{0:T(128)S(1)}, u32[32]{0:T(128)}, u32[]{:S(2)}) copy-start(u32[32]{0:T(128)} %constant.104) | copy-start | bytes 388
  36.2 47.5 %copy-start.17 = (f32[1024]{0:T(1024)S(1)}, f32[1024]{0:T(1024)}, u32[]{:S(2)}) copy-start(f32[1024]{0:T(1024)} %param.16) | copy-start | bytes 12292
  37.2 49.5 %copy-start.1 = (bf16[256,1024]{1,0:T(8,128)(2,1)}, bf16[256,1024]{1,0:T(8,128)(2,1)S(1)}, u32[]{:S(2)}) copy-start(bf16[256,1024]{1,0:T(8,128)(2,1)S(1)} %get-tuple-element.9) | copy-start | bytes 1572868
  37.2 49.5 %copy-start.12 = (f32[256]{0:T(256)}, f32[256]{0:T(256)S(1)}, u32[]{:S(2)}) copy-start(f32[256]{0:T(256)S(1)} %broadcast_multiply_fusion.2) | copy-start | bytes 3076
  37.5 49.2 %copy-start.19 = (f32[256]{0:T(256)}, f32[256]{0:T(256)S(1)}, u32[]{:S(2)}) copy-start(f32[256]{0:T(256)S(1)} %add_rsqrt_fusion) | copy-start | bytes 3076
  87.0 0.9 copy-start.3
  122.2 2.0 copy-start.9
  122.2 2.8 %copy-start.14 = (f32[4]{0:T(128)S(1)}, f32[4]{0:T(128)}, u32[]{:S(2)}) copy-start(f32[4]{0:T(128)} %multiply_reduce_fusion) | copy-start | bytes 52
  122.2 7.4 %copy-start.21 = (bf16[1024,512]{1,0:T(8,128)(2,1)S(1)}, bf16[1024,512]{1,0:T(8,128)(2,1)}, u32[]{:S(2)}) copy-start(bf16[1024,512]{1,0:T(8,128)(2,1)} %all-gather.5.cloned.1.call-done) | copy-start | bytes 3145732
  124.2 3.5 %copy-start.10 = (f32[1024]{0:T(1024)}, f32[1024]{0:T(1024)S(1)}, u32[]{:S(2)}) copy-start(f32[1024]{0:T(1024)S(1)} %broadcast_multiply_fusion.1) | copy-start | bytes 12292
  127.5 0.6 copy-start.15
  131.8 1.6 copy-start.4
  134.6 1.0 copy-start.2
  134.6 1.0 copy-start.13
  134.6 1.0 copy-start.18
  134.6 1.0 copy-start.20
  135.6 1.2 copy-start.5
  139.4 71.5 %copy-start.11 = (f32[1024]{0:T(1024)S(1)}, f32[1024]{0:T(1024)}, u32[]{:S(2)}) copy-start(f32[1024]{0:T(1024)} %copy-done.10) | copy-start | bytes 12292
  139.4 71.5 %copy-start.16 = (f32[4]{0:T(128)S(1)}, f32[4]{0:T(128)}, u32[]{:S(2)}) copy-start(f32[4]{0:T(128)} %copy-done.15) | copy-start | bytes 52
  139.4 111.2 %all-reduce.7.cloned.1.call-start = ((), (), s32[]{:S(2)}) async-start(), calls=%async_computation.4 | async-start | bytes 524288 | tf_op jit(solution)/shard_map/psum | solution.py:134
Sparse Core Ops, SparseCore 0:
  32.6 25.9 all-reduce.8
  211.0 22.3 all-reduce.6
Sparse Core Ops, SparseCore 1:
  35.5 48.1 all-gather.2
  85.9 36.2 all-gather.4
  139.5 71.3 reduce-scatter.1
where the time goes:
time: 262 us; the launch traced here: 261 us
  waiting for transfers between devices  148 us (56%)
  blocking collectives  39.6 us (15%)
  local copies, waits for them, and re-layouts  30.1 us (11%)
  matrix products  17.1 us (7%)
  between operations  16.1 us (6%)
  other arithmetic  10.1 us (4%)
    reduce_scatter x1, waiting for transfers between devices, local(): lax.psum_scatter(jnp.concatenate([first, second], axis=1).astype(jnp.bflo...  71.4 us
    psum x1, blocking collectives, local(): lax.psum(jnp.dot(pooled.T, logit_slope, precision=highest), ('dp', 'vol'))  39.6 us
    all_gather x1, waiting for transfers between devices, local(): out_whole = lax.all_gather(project_out, 'dp', axis=0, tiled=True)  32.9 us
    all_gather x1, waiting for transfers between devices, local(): lax.all_gather(project_in, 'dp', axis=0, tiled=True)  22.6 us
    unnamed x6, waiting for transfers between devices  21 us
    gather x1, local copies, waits for them, and re-layouts, render(): picked = jnp.take(table, rows.reshape(-1), axis=0)[:, ::2]  11.4 us
    slice x1, local copies, waits for them, and re-layouts, render(): picked = jnp.take(table, rows.reshape(-1), axis=0)[:, ::2]  10.3 us
  transfers between devices with their start and end apart: 5, of which 4 were waited for; matrix products, arithmetic and copies ran while one was open for 5% of the time, Pallas kernels for 0%

commit v1 on v0

--- a/solution.py
+++ b/solution.py
@@ -110,7 +110,9 @@
     chances = raised / jnp.sum(raised, axis=1, keepdims=True)
     expected = jnp.sum(chances * errors, axis=1, keepdims=True)
     logit_slope = chances * (errors - expected)
-    head_gradient = lax.psum(jnp.dot(pooled.T, logit_slope, precision=highest), ("dp", "vol"))
+    head_gradient = jnp.sum(
+        lax.all_gather(jnp.dot(pooled.T, logit_slope, precision=highest), ("dp", "vol")), axis=0
+    )
     pooled_slope = jnp.dot(logit_slope, head_weight.T, precision=highest) / PATCHES
     layer_slope = jnp.broadcast_to(pooled_slope[:, None, :], (count, PATCHES, width))
     layer_slope = layer_slope.reshape(count * PATCHES, width).astype(jnp.bfloat16)

time: 262 us -> 291 us (1.11)
  blocking collectives: 39.6 us -> 67.7 us
    all_gather x0 -> x1, blocking collectives: none -> 67.7 us  [local(): lax.all_gather(jnp.dot(pooled.T, logit_slope, precision=highest), ('dp',...]
    psum x1 -> x0, blocking collectives: 39.6 us -> none  [local(): lax.psum(jnp.dot(pooled.T, logit_slope, precision=highest), ('dp', 'vol'))]
where the time goes in v1:
time: 291 us; the launch traced here: 290 us
  waiting for transfers between devices  147 us (51%)
  blocking collectives  67.7 us (23%)
  local copies, waits for them, and re-layouts  30.7 us (11%)
  matrix products  17.1 us (6%)
  between operations  16.1 us (6%)
  other arithmetic  11.1 us (4%)
    reduce_scatter x1, waiting for transfers between devices, local(): lax.psum_scatter(jnp.concatenate([first, second], axis=1).astype(jnp.bflo...  70.7 us
    all_gather x1, blocking collectives, local(): lax.all_gather(jnp.dot(pooled.T, logit_slope, precision=highest), ('dp',...  67.7 us
    all_gather x1, waiting for transfers between devices, local(): out_whole = lax.all_gather(project_out, 'dp', axis=0, tiled=True)  32.9 us
    all_gather x1, waiting for transfers between devices, local(): lax.all_gather(project_in, 'dp', axis=0, tiled=True)  22.6 us
    unnamed x6, waiting for transfers between devices  21 us
    gather x1, local copies, waits for them, and re-layouts, render(): picked = jnp.take(table, rows.reshape(-1), axis=0)[:, ::2]  11.4 us
    slice x1, local copies, waits for them, and re-layouts, render(): picked = jnp.take(table, rows.reshape(-1), axis=0)[:, ::2]  10.3 us
  transfers between devices with their start and end apart: 5, of which 4 were waited for; matrix products, arithmetic and copies ran while one was open for 5% of the time, Pallas kernels for 0%

profile of v1, /device:TPU:0, one launch (start us, length us, event | category | flops | bytes accessed | tf_op | source)
XLA Modules:
  0.0 290.4 jit_solution(14205060143389315861)
XLA Ops:
  8.1 0.7 fusion.38
  8.8 0.7 compare_and_fusion.1
  9.5 11.4 %gather_fusion = bf16[1024,256]{1,0:T(8,128)(2,1)S(1)} fusion(bf16[32768,256]{1,0:T(8,128)(2,1)} %bitcast.112, s32[1024]{0:T(1024)S(1)} %broadcast_clamp_fusion), kind=kCustom, calls=%fused_computation | custom fusion | bytes 1052672 | tf_op jit(solution)/shard_map/jit(_take)/gather | solution.py:67
  21.2 10.3 %slice.21 = bf16[1024,128]{1,0:T(8,128)(2,1)S(1)} slice(bf16[1024,256]{1,0:T(8,128)(2,1)S(1)} %broadcast_select_fusion), slice={[0:1024:1], [0:256:2]} | slice | bytes 524288 | tf_op jit(solution)/shard_map/slice | solution.py:67
  31.7 0.8 convert_element_type.102
  35.6 0.6 convert_element_type.105
  37.5 0.6 dynamic-slice
  38.1 0.6 fusion.9
  38.7 19.9 %all-reduce.9.cloned.1.call-done = bf16[2,65536]{1,0:T(2,128)(2,1)} async-done(((bf16[2,65536]{1,0:T(2,128)(2,1)}), bf16[2,65536]{1,0:T(2,128)(2,1)}) %all-reduce.9.cloned.1.call-update) | async-done | bytes 262160
  58.6 1.8 dynamic-slice_convert_fusion
  60.4 0.6 multiply_reduce_fusion
  61.0 22.6 %all-gather.4.cloned.1.call-done = bf16[1024,1536]{1,0:T(8,128)(2,1)} async-done(((bf16[64,1536]{1,0:T(8,128)(2,1)}), bf16[1024,1536]{1,0:T(8,128)(2,1)}) %all-gather.4.cloned.1.call-update) | async-done | bytes 3145744 | tf_op jit(solution)/shard_map/all_gather | solution.py:99
  83.7 3.0 %convolution_convert_fusion.1 = bf16[256,1536]{1,0:T(8,128)(2,1)S(1)} fusion(bf16[1024,1536]{1,0:T(8,128)(2,1)} %all-gather.4.cloned.1.call-done, bf16[256,1024]{1,0:T(8,128)(2,1)S(1)} %get-tuple-element.9, f32[1024]{0:T(1024)S(1)} %copy-done.17, f32[256]{0:T(256)S(1)} %add_rsqrt_fusion, f32[256]{0:T(256)S(1)} %broadcast_multiply_fusion.2), kind=kOutput, calls=%fused_computation.5 | convolution fusion | flops 807010304 | bytes 4462592 | tf_op jit(solution)/shard_map/dot_general | solution.py:97
  88.0 1.2 convolution_convert_fusion.5
  89.3 32.9 %all-gather.6.cloned.1.call-done = bf16[1024,512]{1,0:T(8,128)(2,1)} async-done(((bf16[64,512]{1,0:T(8,128)(2,1)}), bf16[1024,512]{1,0:T(8,128)(2,1)}) %all-gather.6.cloned.1.call-update) | async-done | bytes 1048592 | tf_op jit(solution)/shard_map/all_gather | solution.py:104
  122.2 1.9 fusion.8
  124.2 0.8 fusion.64
  125.0 1.3 multiply_reduce_fusion.1
  126.3 1.2 subtract_multiply_fusion
  128.1 1.5 convolution_convert_fusion.3
  129.6 1.1 convolution_convert_fusion.4
  130.7 1.1 copy.42
  131.8 1.5 fusion.4
  134.0 0.6 convolution_bitcast_fusion.1
  135.6 1.2 convolution_convert_fusion
  136.8 2.6 pad_maximum_fusion
  139.5 0.6 copy-done.11
  140.2 70.7 %reduce-scatter.2.cloned.1.call-done = bf16[64,2048]{1,0:T(8,128)(2,1)} async-done(((bf16[1024,2048]{1,0:T(8,128)(2,1)}), bf16[64,2048]{1,0:T(8,128)(2,1)}) %reduce-scatter.2.cloned.1.call-update) | async-done | bytes 262160 | tf_op jit(solution)/shard_map/reduce_scatter | solution.py:130
  210.9 67.7 %all-gather = f32[32768,4]{0,1:T(4,128)S(1)} all-gather(f32[1024,4]{0,1:T(4,128)S(1)} %broadcast_multiply_fusion), channel_id=2, replica_groups=mesh['dp'=16,'vol'=2] {'dp','vol'}, dimensions={0}, use_global_device_ids=true | all-gather | bytes 540672 | tf_op jit(solution)/shard_map/all_gather | solution.py:114
  278.7 0.9 bitcast_reduce_fusion
  279.6 1.7 slice.32
  281.3 1.5 slice.33
  (85 shorter events, 8.4 us)
Async XLA Ops:
  8.0 28.7 %copy-start = (bf16[64,1024]{1,0:T(8,128)(2,1)S(1)}, bf16[64,1024]{1,0:T(8,128)(2,1)}, u32[]{:S(2)}) copy-start(bf16[64,1024]{1,0:T(8,128)(2,1)} %param.14) | copy-start | bytes 393220
  8.0 50.5 %all-reduce.9.cloned.1.call-start = ((), (), s32[]{:S(2)}) async-start(), calls=%async_computation.5 | async-start | bytes 524288
  20.9 13.0 %copy-start.7 = (f32[1,128,128]{2,1,0:T(8,128)S(1)}, f32[1,128,128]{2,1,0:T(8,128)}, u32[]{:S(2)}) copy-start(f32[1,128,128]{2,1,0:T(8,128)} %param.10) | copy-start | bytes 196612
  21.0 14.6 %copy-start.8 = (bf16[1,128,128]{2,1,0:T(8,128)(2,1)S(1)}, bf16[1,128,128]{2,1,0:T(8,128)(2,1)}, u32[]{:S(2)}) copy-start(bf16[1,128,128]{2,1,0:T(8,128)(2,1)} %param.11) | copy-start | bytes 98308
  31.5 5.3 %copy-start.6 = (bf16[256,1024]{1,0:T(8,128)(2,1)S(1)}, bf16[256,1024]{1,0:T(8,128)(2,1)}, u32[]{:S(2)}) copy-start(bf16[256,1024]{1,0:T(8,128)(2,1)} %param.15) | copy-start | bytes 1572868
  32.5 51.2 %all-gather.4.cloned.1.call-start = ((), (), s32[]{:S(2)}) async-start(), calls=%async_computation.1 | async-start | bytes 3342336 | tf_op jit(solution)/shard_map/all_gather | solution.py:99
  33.1 89.2 %all-gather.6.cloned.1.call-start = ((), (), s32[]{:S(2)}) async-start(), calls=%async_computation.2 | async-start | bytes 1114112 | tf_op jit(solution)/shard_map/all_gather | solution.py:104
  33.6 177.2 %reduce-scatter.2.cloned.1.call-start = ((), (), s32[]{:S(2)}) async-start(), calls=%async_computation.3 | async-start | bytes 4456448 | tf_op jit(solution)/shard_map/reduce_scatter | solution.py:130
  34.4 3.1 %copy-start.22 = (u32[32]{0:T(128)S(1)}, u32[32]{0:T(128)}, u32[]{:S(2)}) copy-start(u32[32]{0:T(128)} %constant.104) | copy-start | bytes 388
  36.2 47.5 %copy-start.17 = (f32[1024]{0:T(1024)S(1)}, f32[1024]{0:T(1024)}, u32[]{:S(2)}) copy-start(f32[1024]{0:T(1024)} %param.16) | copy-start | bytes 12292
  37.2 49.5 %copy-start.1 = (bf16[256,1024]{1,0:T(8,128)(2,1)}, bf16[256,1024]{1,0:T(8,128)(2,1)S(1)}, u32[]{:S(2)}) copy-start(bf16[256,1024]{1,0:T(8,128)(2,1)S(1)} %get-tuple-element.9) | copy-start | bytes 1572868
  37.2 49.5 %copy-start.12 = (f32[256]{0:T(256)}, f32[256]{0:T(256)S(1)}, u32[]{:S(2)}) copy-start(f32[256]{0:T(256)S(1)} %broadcast_multiply_fusion.2) | copy-start | bytes 3076
  37.5 49.2 %copy-start.19 = (f32[256]{0:T(256)}, f32[256]{0:T(256)S(1)}, u32[]{:S(2)}) copy-start(f32[256]{0:T(256)S(1)} %add_rsqrt_fusion) | copy-start | bytes 3076
  87.0 0.9 copy-start.3
  122.2 2.0 copy-start.9
  122.2 2.8 copy-start.14
  122.2 7.4 %copy-start.21 = (bf16[1024,512]{1,0:T(8,128)(2,1)S(1)}, bf16[1024,512]{1,0:T(8,128)(2,1)}, u32[]{:S(2)}) copy-start(bf16[1024,512]{1,0:T(8,128)(2,1)} %all-gather.6.cloned.1.call-done) | copy-start | bytes 3145732
  124.2 3.5 %copy-start.10 = (f32[1024]{0:T(1024)}, f32[1024]{0:T(1024)S(1)}, u32[]{:S(2)}) copy-start(f32[1024]{0:T(1024)S(1)} %broadcast_multiply_fusion.1) | copy-start | bytes 12292
  127.5 0.6 copy-start.15
  131.8 1.6 copy-start.4
  134.6 1.0 copy-start.2
  134.6 1.0 copy-start.13
  134.6 1.0 copy-start.18
  134.6 1.0 copy-start.20
  135.6 1.2 copy-start.5
  139.4 0.7 copy-start.11
  139.4 0.7 copy-start.16
  139.4 140.1 %all-reduce.7.cloned.1.call-start = ((), (), s32[]{:S(2)}) async-start(), calls=%async_computation.4 | async-start | bytes 524288 | tf_op jit(solution)/shard_map/psum | solution.py:136
Sparse Core Ops, SparseCore 0:
  32.6 25.9 all-reduce.8
  211.0 23.0 all-reduce.6
Sparse Core Ops, SparseCore 1:
  35.5 48.1 all-gather.3
  85.9 36.2 all-gather.5
  139.5 71.3 reduce-scatter.1
